TPU v7x, 1024 devices: a whole 4x4x32 slice. The times are simulated.
1024 devices in a mesh: frames: 16 (over x_hi, y, core), rows: 64 (over x_lo, z).
Axes of the slice: x: 4 (x_hi: 2, x_lo: 2; x = x_hi * 2 + x_lo), y: 4, z: 32, core: 2. Of those that a mesh axis runs over, the one named last changes fastest.
Arguments:
- fine_q: bfloat16 [16, 512, 16, 256], P('frames', 'rows'), may hold values from -24 to 24
- fine_kv: bfloat16 [16, 512, 16, 512], P('frames', 'rows'), may hold values from -24 to 24
- coarse_q: bfloat16 [16, 64, 2, 1024], P('frames', 'rows'), may hold values from -24 to 24
- coarse_kv: bfloat16 [16, 64, 2, 2048], P('frames', 'rows'), may hold values from -24 to 24
- cotangent: bfloat16 [16, 512, 16, 256], P('frames', 'rows'), may hold values from -6 to 6
- gain_table: float32 [1000, 256], replicated, may hold values from 0.3 to 3
- timesteps: int32 [16], P('frames'), may hold values from 0 to 999
- valid_cols: int32 [16], replicated, may hold values from 8 to 16
Outputs:
- grad_fine_q: bfloat16 [16, 512, 16, 256], P('frames', 'rows')
- grad_fine_kv: bfloat16 [16, 512, 16, 512], P('frames', 'rows')
- grad_coarse_q: bfloat16 [16, 64, 2, 1024], P(None, 'rows', None, 'frames')
- grad_coarse_k: bfloat16 [16, 64, 2, 1024], P(None, 'rows', None, 'frames')
- grad_coarse_v: bfloat16 [16, 64, 2, 1024], P(None, 'rows', None, 'frames')
All inputs are finite; a program needn't handle non-finite values.
Results may differ from a plain program's by a relative error of at most 0.023.
Values may be sent and summed in bfloat16 or wider, within the bound.
A program may use at most 32 MiB of HBM per device.

v0:
```python
import math

import jax
import jax.numpy as jnp
from jax import lax
from jax.sharding import PartitionSpec as P

HD = 64
KERNEL = 7
POOL = 8


NEGATIVE = -1e30


def passed_along(value, axis, steps):
    count = lax.axis_size(axis)
    initial, last = (max(0, -steps), min(count, count - steps))
    return lax.ppermute(value, axis, [(source, source + steps) for source in range(initial, last)])


def extended(cells, sides, width):
    for axis, dim in sides:
        count = lax.axis_size(axis)
        ends = count - 1
        head = lax.slice_in_dim(cells, 0, width, axis=dim)
        tail = lax.slice_in_dim(cells, cells.shape[dim] - width, cells.shape[dim], axis=dim)
        cells = jnp.concatenate(
            [
                lax.ppermute(tail, axis, [(i, (i + 1) % count) for i in range(ends)]),
                cells,
                lax.ppermute(head, axis, [((i + 1) % count, i) for i in range(ends)]),
            ],
            axis=dim,
        )
    return cells


def normalize(scores):
    row_max = jnp.max(scores, axis=-1, keepdims=True)
    return row_max + jnp.log(jnp.sum(jnp.exp(scores - row_max), axis=-1, keepdims=True))


def pass_rim(rim, offset):
    return passed_along(rim.astype(jnp.bfloat16), "rows", offset).astype(rim.dtype)


def local(fine_q, fine_kv, coarse_q, coarse_kv, cotangent, gain_table, timesteps, valid_cols):
    score_scale = 1.0 / math.sqrt(HD)
    frame_dev = lax.axis_index("frames")
    row_dev = lax.axis_index("rows")
    row_devices = lax.axis_size("rows")
    frames_here, rows_here, cols_here, fine_width = fine_q.shape
    head_count = fine_width // HD
    radius = KERNEL // 2
    band_rows = rows_here + 2 * radius
    total_frames = valid_cols.shape[0]
    steps_all = gain_table.shape[0]
    tile_cols = 16
    tile_count = cols_here // tile_cols
    tile_keys = tile_cols + 2 * radius
    both_width = 2 * fine_width
    select = (timesteps[:, None] == jnp.arange(steps_all)[None, :]).astype(jnp.float32)
    frame_gain = jnp.dot(select, gain_table, precision=lax.Precision.HIGHEST)
    scaled_grad = frame_gain[:, None, None, :] * cotangent.astype(jnp.float32)
    grad_low = scaled_grad.astype(jnp.bfloat16)
    frame_ids = frame_dev * frames_here + jnp.arange(frames_here)
    frame_match = frame_ids[:, None] == jnp.arange(total_frames)[None, :]
    valid_here = jnp.sum(jnp.where(frame_match, valid_cols[None, :], 0), axis=1)
    half_pool = POOL // 2
    coarse_cols = cols_here // POOL
    coarse_width = coarse_q.shape[-1]
    coarse_count = frames_here * coarse_cols
    blocks = scaled_grad.reshape(frames_here, 2, half_pool, coarse_cols, 2, half_pool, fine_width)
    pooled = (
        jnp.sum(blocks, axis=(2, 5))
        .transpose(0, 2, 1, 3, 4)
        .reshape(coarse_count, coarse_width)
        .astype(jnp.bfloat16)
    )
    mine_query = coarse_q.reshape(coarse_count, coarse_width)
    mine_keys = coarse_kv[..., :coarse_width].reshape(coarse_count, coarse_width)
    mine_values = coarse_kv[..., coarse_width:].reshape(coarse_count, coarse_width)
    head_query, head_keys, head_values, head_grad = (
        lax.all_to_all(mine_query, "frames", split_axis=1, concat_axis=0, tiled=True),
        lax.all_to_all(mine_keys, "frames", split_axis=1, concat_axis=0, tiled=True),
        lax.all_to_all(mine_values, "frames", split_axis=1, concat_axis=0, tiled=True),
        lax.all_to_all(pooled, "frames", split_axis=1, concat_axis=0, tiled=True),
    )
    padded = extended(fine_kv, (("rows", 1),), radius)
    widened = jnp.pad(padded, ((0, 0), (0, 0), (radius, tile_cols - radius), (0, 0)))
    main_cols = widened[:, :, :cols_here].reshape(
        frames_here, band_rows, tile_count, tile_cols, both_width
    )
    extra_cols = widened[:, :, tile_cols:].reshape(
        frames_here, band_rows, tile_count, tile_cols, both_width
    )[:, :, :, : 2 * radius]
    kv_tiles = jnp.concatenate([main_cols, extra_cols], axis=3).transpose(0, 2, 1, 3, 4)
    key_count = band_rows * tile_keys
    query_count = rows_here * tile_cols
    kv_tiles = kv_tiles.reshape(frames_here, tile_count, key_count, both_width)
    key_wide = kv_tiles[..., :fine_width].reshape(
        frames_here, tile_count, key_count, head_count, HD
    )
    value_wide = kv_tiles[..., fine_width:].reshape(
        frames_here, tile_count, key_count, head_count, HD
    )

    def to_tiles(table):
        return (
            table.reshape(frames_here, rows_here, tile_count, tile_cols, fine_width)
            .transpose(0, 2, 1, 3, 4)
            .reshape(frames_here, tile_count, query_count, head_count, HD)
        )

    query_wide = to_tiles(fine_q)
    grad_wide = to_tiles(grad_low)
    query_index = jnp.arange(query_count)
    key_index = jnp.arange(key_count)
    query_row = query_index // tile_cols
    query_col = query_index % tile_cols
    key_row = key_index // tile_keys - radius
    key_col = key_index % tile_keys - radius
    row_gap = key_row[None, :] - query_row[:, None]
    col_gap = key_col[None, :] - query_col[:, None]
    key_global = row_dev * rows_here + key_row
    nearby = (
        (jnp.abs(row_gap) <= radius)
        & (jnp.abs(col_gap) <= radius)
        & ((key_global >= 0) & (key_global < rows_here * row_devices))[None, :]
    )
    centre = (row_gap == 0) & (col_gap == 0)
    col_global = jnp.arange(tile_count)[:, None] * tile_cols + key_col[None, :]
    col_fine = (col_global >= 0) & (col_global < cols_here)
    col_valid = col_fine[None] & (col_global[None] < valid_here[:, None, None])
    allowed = nearby[None, None] & col_valid[:, :, None, :] | centre[None, None]
    scores = (
        jnp.einsum("fnqhd,fnkhd->fnhqk", query_wide, key_wide, preferred_element_type=jnp.float32)
        * score_scale
    )
    scores = jnp.where(allowed[:, :, None], scores, NEGATIVE)
    weights = jnp.exp(scores - normalize(scores))
    weights_low = weights.astype(jnp.bfloat16)
    attended = jnp.einsum(
        "fnhqk,fnkhd->fnqhd", weights_low, value_wide, preferred_element_type=jnp.float32
    )
    row_dot = jnp.sum(grad_wide.astype(jnp.float32) * attended, axis=-1)
    weight_grad = jnp.einsum(
        "fnqhd,fnkhd->fnhqk", grad_wide, value_wide, preferred_element_type=jnp.float32
    )
    score_grad = (weights * (weight_grad - jnp.moveaxis(row_dot, 3, 2)[..., None])).astype(
        jnp.bfloat16
    )
    query_grad = (
        jnp.einsum("fnhqk,fnkhd->fnqhd", score_grad, key_wide, preferred_element_type=jnp.float32)
        * score_scale
    )
    key_grad = (
        jnp.einsum("fnhqk,fnqhd->fnkhd", score_grad, query_wide, preferred_element_type=jnp.float32)
        * score_scale
    )
    value_grad = jnp.einsum(
        "fnhqk,fnqhd->fnkhd", weights_low, grad_wide, preferred_element_type=jnp.float32
    )
    grad_fine_q = (
        query_grad.reshape(frames_here, tile_count, rows_here, tile_cols, fine_width)
        .transpose(0, 2, 1, 3, 4)
        .reshape(frames_here, rows_here, cols_here, fine_width)
        .astype(jnp.bfloat16)
    )
    tile_grads = jnp.concatenate(
        [
            key_grad.reshape(frames_here, tile_count, band_rows, tile_keys, fine_width),
            value_grad.reshape(frames_here, tile_count, band_rows, tile_keys, fine_width),
        ],
        axis=-1,
    )
    tile_grads = tile_grads.transpose(0, 2, 1, 3, 4)
    main_part = tile_grads[:, :, :, :tile_cols].reshape(
        frames_here, band_rows, cols_here, both_width
    )
    extra_part = jnp.pad(
        tile_grads[:, :, :, tile_cols:],
        ((0, 0), (0, 0), (0, 0), (0, tile_cols - 2 * radius), (0, 0)),
    ).reshape(frames_here, band_rows, cols_here, both_width)
    summed_cols = jnp.zeros(
        (frames_here, band_rows, cols_here + tile_cols, both_width), jnp.float32
    )
    summed_cols = (
        summed_cols.at[:, :, :cols_here].add(main_part).at[:, :, tile_cols:].add(extra_part)
    )
    key_value = summed_cols[:, :, radius : radius + cols_here]
    owned_rows = key_value[:, radius : radius + rows_here]
    from_below = pass_rim(key_value[:, :radius], -1)
    from_above = pass_rim(key_value[:, radius + rows_here :], 1)
    owned_rows = (
        owned_rows.at[:, :radius].add(from_above).at[:, rows_here - radius :].add(from_below)
    )
    grad_fine_kv = owned_rows.astype(jnp.bfloat16)
    head_tokens, head_width = head_query.shape
    head_groups = head_width // HD
    query_heads = head_query.reshape(head_tokens, head_groups, HD)
    grad_heads = head_grad.reshape(head_tokens, head_groups, HD)
    every_keys, every_values = (
        lax.all_gather(head_keys, "rows", axis=0, tiled=True),
        lax.all_gather(head_values, "rows", axis=0, tiled=True),
    )
    every_count = every_keys.shape[0]
    key_heads = every_keys.reshape(every_count, head_groups, HD)
    value_heads = every_values.reshape(every_count, head_groups, HD)
    position = jnp.arange(every_count) % head_tokens
    key_frame = position // coarse_cols
    key_column = position % coarse_cols
    col_limit = jnp.sum(
        jnp.where(key_frame[:, None] == jnp.arange(total_frames)[None, :], valid_cols[None, :], 0),
        axis=1,
    )
    key_ok = key_column * POOL < col_limit
    coarse_scores = (
        jnp.einsum("qhd,khd->hqk", query_heads, key_heads, preferred_element_type=jnp.float32)
        * score_scale
    )
    coarse_scores = jnp.where(key_ok[None, None, :], coarse_scores, NEGATIVE)
    log_total = normalize(coarse_scores)
    coarse_weights = jnp.exp(coarse_scores - log_total)
    coarse_low = coarse_weights.astype(jnp.bfloat16)
    coarse_out = jnp.einsum(
        "hqk,khd->qhd", coarse_low, value_heads, preferred_element_type=jnp.float32
    )
    coarse_dot = jnp.sum(grad_heads.astype(jnp.float32) * coarse_out, axis=-1)
    coarse_wgrad = jnp.einsum(
        "qhd,khd->hqk", grad_heads, value_heads, preferred_element_type=jnp.float32
    )
    coarse_sgrad = (coarse_weights * (coarse_wgrad - coarse_dot.T[:, :, None])).astype(jnp.bfloat16)
    coarse_qgrad = (
        jnp.einsum("hqk,khd->qhd", coarse_sgrad, key_heads, preferred_element_type=jnp.float32)
        * score_scale
    )
    count = head_tokens * lax.axis_size("rows")
    key_part = (
        jnp.einsum("hqk,qhd->khd", coarse_sgrad, query_heads, preferred_element_type=jnp.float32)
        * score_scale
    )
    value_part = jnp.einsum(
        "hqk,qhd->khd", coarse_low, grad_heads, preferred_element_type=jnp.float32
    )
    terms = lax.psum_scatter(
        jnp.concatenate(
            [key_part.reshape(count, head_width), value_part.reshape(count, head_width)], axis=1
        ),
        "rows",
        scatter_dimension=0,
        tiled=True,
    )
    total_keys = terms[:, :head_width]
    total_values = terms[:, head_width:]
    out_dims = (head_tokens // coarse_cols, 1, coarse_cols, head_width)
    grad_coarse_q = coarse_qgrad.reshape(out_dims).astype(jnp.bfloat16)
    grad_coarse_k = total_keys.reshape(out_dims).astype(jnp.bfloat16)
    grad_coarse_v = total_values.reshape(out_dims).astype(jnp.bfloat16)
    return (grad_fine_q, grad_fine_kv, grad_coarse_q, grad_coarse_k, grad_coarse_v)


def solution(mesh):
    placed = (
        P("frames", "rows", None, None),
        P("frames", "rows", None, None),
        P("frames", "rows", None, None),
        P("frames", "rows", None, None),
        P("frames", "rows", None, None),
        P(),
        P("frames"),
        P(),
    )
    return jax.shard_map(
        local,
        mesh=mesh,
        in_specs=placed,
        out_specs=(
            P("frames", "rows", None, None),
            P("frames", "rows", None, None),
            P(None, "rows", None, "frames"),
            P(None, "rows", None, "frames"),
            P(None, "rows", None, "frames"),
        ),
        check_vma=False,
    )
```

profile of v0, /device:TPU:8, one launch (start us, length us, event | category | flops | bytes accessed | tf_op | source)
XLA Modules:
  0.0 571.8 jit_solution(13355572277159263226)
XLA Ops:
  7.2 0.9 fusion.60
  8.1 1.3 collective-permute-start.1
  9.4 4.5 collective-permute-start
  14.1 0.6 copy.98
  14.7 16.4 %all-to-all-start.1 = ((bf16[2,16,64]{2,0,1:T(2,128)(2,1)}), bf16[2,16,64]{2,0,1:T(2,128)(2,1)S(1)}, u32[]{:S(2)}, u32[]{:S(2)}) async-start(bf16[2,16,64]{2,0,1:T(2,128)(2,1)} %copy.98), calls=%async_computation.1 | async-start | bytes 16384 | tf_op jit(solution)/shard_map/all_to_all | solution.py:86
  31.8 0.6 copy-done.6
  32.4 0.6 fusion.55
  34.0 0.7 compare_and_fusion
  35.4 0.7 copy-done.2
  36.7 0.6 copy.100
  37.4 0.6 copy.101
  38.1 0.6 copy.97
  38.7 7.3 %all-to-all-start = ((bf16[2,16,64]{2,0,1:T(2,128)(2,1)}), bf16[2,16,64]{2,0,1:T(2,128)(2,1)S(1)}, u32[]{:S(2)}, u32[]{:S(2)}) async-start(bf16[2,16,64]{2,0,1:T(2,128)(2,1)} %copy.97), calls=%async_computation | async-start | bytes 16384 | tf_op jit(solution)/shard_map/all_to_all | solution.py:85
  46.0 125.0 %all_gather.6 = bf16[2048,64]{1,0:T(8,128)(2,1)S(1)} all-gather(bf16[32,64]{1,0:T(8,128)(2,1)S(1)} %bitcast.143), channel_id=1, replica_groups=mesh['frames'=16,'rows'=64] {'rows'}, dimensions={0}, use_global_device_ids=true | all-gather | bytes 266240 | tf_op jit(solution)/shard_map/all_gather | solution.py:205
  171.0 7.8 %all-to-all-start.3 = ((bf16[2,16,64]{2,0,1:T(2,128)(2,1)}), bf16[2,16,64]{2,0,1:T(2,128)(2,1)S(1)}, u32[]{:S(2)}, u32[]{:S(2)}) async-start(bf16[2,16,64]{2,0,1:T(2,128)(2,1)} %copy.101), calls=%async_computation.3 | async-start | bytes 16384 | tf_op jit(solution)/shard_map/all_to_all | solution.py:87
  179.5 5.5 all-to-all-done.3
  185.0 4.7 all-to-all-start.2
  189.8 119.4 %all_gather.7 = bf16[2048,64]{1,0:T(8,128)(2,1)S(1)} all-gather(bf16[32,64]{1,0:T(8,128)(2,1)S(1)} %bitcast.144), channel_id=1, replica_groups=mesh['frames'=16,'rows'=64] {'rows'}, dimensions={0}, use_global_device_ids=true | all-gather | bytes 266240 | tf_op jit(solution)/shard_map/all_gather | solution.py:206
  310.5 0.8 fusion.13
  311.3 1.3 copy.107
  312.6 0.9 copy-done.1
  315.2 0.6 reshape.711
  317.0 0.6 reshape.710
  319.0 1.0 maximum_convert_fusion
  320.3 3.4 collective-permute-start.2
  324.3 0.8 convert_element_type.155
  325.1 1.3 collective-permute-start.3
  326.6 5.0 collective-permute-done.3
  332.0 0.7 copy.103
  332.7 230.9 %reduce-scatter.4.cloned.1.call-done = f32[32,128]{1,0:T(8,128)} async-done(((f32[2048,128]{1,0:T(8,128)}), f32[32,128]{1,0:T(8,128)}) %reduce-scatter.4.cloned.1.call-update) | async-done | bytes 16400 | tf_op jit(solution)/shard_map/reduce_scatter | solution.py:247
  563.5 0.7 convert.11
  564.3 0.7 fusion.61
  (79 shorter events, 10.1 us)
Async XLA Ops:
  7.2 26.0 %copy-start = (f32[1000,256]{1,0:T(8,128)S(1)}, f32[1000,256]{1,0:T(8,128)}, u32[]{:S(2)}) copy-start(f32[1000,256]{1,0:T(8,128)} %param.21) | copy-start | bytes 3072004
  7.2 6.8 %copy-start.4 = (bf16[1,1,2,2048]{3,2,1,0:T(2,128)(2,1)S(1)}, bf16[1,1,2,2048]{3,2,1,0:T(2,128)(2,1)}, u32[]{:S(2)}) copy-start(bf16[1,1,2,2048]{3,2,1,0:T(2,128)(2,1)} %param.19) | copy-start | bytes 24580
  8.1 304.5 %collective-permute-start.1 = (bf16[1,3,16,512]{3,2,1,0:T(8,128)(2,1)S(1)}, bf16[1,3,16,512]{3,2,1,0:T(8,128)(2,1)S(1)}, u32[]{:S(2)}, u32[]{:S(2)}) collective-permute-start(bf16[1,3,16,512]{3,2,1,0:T(8,128)(2,1)S(1)} %get-tuple-element.85), channel_id=1, source_target_pairs={{1,0},{2,1},{3,2},{4,3},{5,4},{6,5},{7,6},{8,7},{9,8},{10,9},{11,1... | collective-permute-start | bytes 147464 | tf_op jit(solution)/shard_map/ppermute | solution.py:32
  9.4 303.2 %collective-permute-start = (bf16[1,3,16,512]{3,2,1,0:T(8,128)(2,1)S(1)}, bf16[1,3,16,512]{3,2,1,0:T(8,128)(2,1)S(1)}, u32[]{:S(2)}, u32[]{:S(2)}) collective-permute-start(bf16[1,3,16,512]{3,2,1,0:T(8,128)(2,1)S(1)} %get-tuple-element.84), channel_id=1, source_target_pairs={{0,1},{1,2},{2,3},{3,4},{4,5},{5,6},{6,7},{7,8},{8,9},{9,10},{10,1... | collective-permute-start | bytes 147464 | tf_op jit(solution)/shard_map/ppermute | solution.py:30
  14.7 24.1 %all-to-all-start.1 = ((bf16[2,16,64]{2,0,1:T(2,128)(2,1)}), bf16[2,16,64]{2,0,1:T(2,128)(2,1)S(1)}, u32[]{:S(2)}, u32[]{:S(2)}) async-start(bf16[2,16,64]{2,0,1:T(2,128)(2,1)} %copy.98), calls=%async_computation.1 | async-start | bytes 16384 | tf_op jit(solution)/shard_map/all_to_all | solution.py:86
  31.8 0.7 copy-start.6
  33.2 0.8 copy-start.3
  35.2 0.8 copy-start.2
  37.3 0.7 copy-start.5
  38.7 132.3 %all-to-all-start = ((bf16[2,16,64]{2,0,1:T(2,128)(2,1)}), bf16[2,16,64]{2,0,1:T(2,128)(2,1)S(1)}, u32[]{:S(2)}, u32[]{:S(2)}) async-start(bf16[2,16,64]{2,0,1:T(2,128)(2,1)} %copy.97), calls=%async_computation | async-start | bytes 16384 | tf_op jit(solution)/shard_map/all_to_all | solution.py:85
  171.0 14.0 %all-to-all-start.3 = ((bf16[2,16,64]{2,0,1:T(2,128)(2,1)}), bf16[2,16,64]{2,0,1:T(2,128)(2,1)S(1)}, u32[]{:S(2)}, u32[]{:S(2)}) async-start(bf16[2,16,64]{2,0,1:T(2,128)(2,1)} %copy.101), calls=%async_computation.3 | async-start | bytes 16384 | tf_op jit(solution)/shard_map/all_to_all | solution.py:87
  185.0 124.2 %all-to-all-start.2 = ((bf16[2,16,64]{2,0,1:T(2,128)(2,1)}), bf16[2,16,64]{2,0,1:T(2,128)(2,1)S(1)}, u32[]{:S(2)}, u32[]{:S(2)}) async-start(bf16[2,16,64]{2,0,1:T(2,128)(2,1)} %copy.100), calls=%async_computation.2 | async-start | bytes 16384 | tf_op jit(solution)/shard_map/all_to_all | solution.py:88
  189.7 373.8 %reduce-scatter.4.cloned.1.call-start = ((), (), s32[]{:S(2)}) async-start(), calls=%async_computation.5 | async-start | bytes 1064960 | tf_op jit(solution)/shard_map/reduce_scatter | solution.py:247
  312.6 0.9 copy-start.1
  320.3 6.1 %collective-permute-start.2 = (bf16[1,3,16,512]{3,0,2,1:T(2,128)(2,1)S(1)}, bf16[1,3,16,512]{3,0,2,1:T(2,128)(2,1)S(1)}, u32[]{:S(2)}, u32[]{:S(2)}) collective-permute-start(bf16[1,3,16,512]{3,0,2,1:T(2,128)(2,1)S(1)} %get-tuple-element.79), channel_id=1, source_target_pairs={{0,1},{1,2},{2,3},{3,4},{4,5},{5,6},{6,7},{7,8},{8,9},{9,10},{10,1... | collective-permute-start | bytes 147464 | tf_op jit(solution)/shard_map/ppermute | solution.py:19
  325.1 6.5 %collective-permute-start.3 = (bf16[1,3,16,512]{3,0,2,1:T(2,128)(2,1)S(1)}, bf16[1,3,16,512]{3,0,2,1:T(2,128)(2,1)S(1)}, u32[]{:S(2)}, u32[]{:S(2)}) collective-permute-start(bf16[1,3,16,512]{3,0,2,1:T(2,128)(2,1)S(1)} %get-tuple-element.78), channel_id=1, source_target_pairs={{1,0},{2,1},{3,2},{4,3},{5,4},{6,5},{7,6},{8,7},{9,8},{10,9},{11,1... | collective-permute-start | bytes 147464 | tf_op jit(solution)/shard_map/ppermute | solution.py:19
Sparse Core Ops, SparseCore 0:
  312.7 250.7 reduce-scatter.3
where the time goes:
time: 572 us
  blocking collectives  244 us (43%)
  waiting for transfers between devices  241 us (42%)
  starting transfers between devices  46.7 us (8%)
  between operations  15.1 us (3%)
  local copies, waits for them, and re-layouts  14.1 us (2%)
    reduce_scatter x1, waiting for transfers between devices, local(): lax.psum_scatter(jnp.concatenate([key_part.reshape(count, head_width), va...  231 us
    all_gather x1, blocking collectives, local(): lax.all_gather(head_keys, 'rows', axis=0, tiled=True)  125 us
    all_gather x1, blocking collectives, local(): lax.all_gather(head_values, 'rows', axis=0, tiled=True)  119 us
    all_to_all x1, starting transfers between devices, local(): lax.all_to_all(mine_keys, 'frames', split_axis=1, concat_axis=0, tiled=True)  16.4 us
  transfers between devices with their start and end apart: 9, of which 3 were waited for; matrix products, arithmetic and copies ran while one was open for 3% of the time, Pallas kernels for 0%

commit v1 on v0

v1 whole, which is shorter than its diff:
```python
import functools

import jax
import jax.numpy as jnp
from jax import lax
from jax.experimental import pallas as pl
from jax.experimental.pallas import tpu as pltpu
from jax.sharding import PartitionSpec as P

F = 16
NZ = 32
ROWS = 64
HALO = 48
PIX = 128
KEYS = PIX + 2 * HALO
TOK = 2048
QT = 256
NEG = -1e30
BF = jnp.bfloat16
F32 = jnp.float32
MESH = pl.DeviceIdType.MESH


def tree():
    children = {0: [3, -3, 1, -1]}
    for k in (3, 6, 9, 12):
        children[k] = [k + 3, k - 1, k + 1]
        children[-k] = [-k - 3, -k + 1, -k - 1]
    children[15] = [16, 14]
    children[-15] = [-14]
    cost = {0: 0.0}
    todo = [0]
    while todo:
        d = todo.pop(0)
        for c in children.get(d, []):
            cost[c] = cost[d] + 0.88 + 0.75 * abs(c - d)
            todo.append(c)
    order = sorted((d for d in cost if d), key=lambda d: (cost[d], -d))
    return children, order


def dot(a, b, ca, cb):
    return lax.dot_general(a, b, (((ca,), (cb,)), ((), ())), preferred_element_type=F32)


def kernel(
    ts, vc, fq_h, fkv_h, cot_h, cq_h, ckv_h, gain_h,
    dfq_h, dfkv_h, dq_h, dk_h, dv_h,
    fq, kv, cot, cq, ckv, gain, stage, land, buf,
    gs, dkv, rim_out, rim_in, a_ref, b_ref, t_ref, ld,
    o_fq, o_fkv, o_q, o_k, o_v,
    in_sem, out_sem, halo_s, halo_r, rim_s, rim_r, a2a_s, a2a_r, self_sem,
    z_s, z_r, x_s, x_r,
):
    f = lax.axis_index("frames")
    r = lax.axis_index("rows")
    xl = r // NZ
    z = lax.rem(r, NZ)

    def zdev(d):
        return (f, xl * NZ + lax.rem(z + d + NZ, NZ))

    xdev = (f, (1 - xl) * NZ + z)
    above = (f, lax.rem(r + ROWS - 1, ROWS))
    below = (f, lax.rem(r + 1, ROWS))

    loads = [
        pltpu.make_async_copy(src, dst, in_sem.at[i])
        for i, (src, dst) in enumerate(
            (
                (cq_h, cq),
                (ckv_h, ckv),
                (gain_h, gain),
                (cot_h, cot),
                (fq_h, fq),
                (fkv_h, kv.at[pl.ds(HALO, PIX)]),
            )
        )
    ]
    for c in loads:
        c.start()

    barrier = pltpu.get_barrier_semaphore()
    peers = [(lax.rem(f + k, F), r) for k in range(1, F)]
    peers += [zdev(1), zdev(-1), zdev(3), zdev(-3), xdev, above, below]
    for peer in peers:
        pl.semaphore_signal(barrier, inc=1, device_id=peer, device_id_type=MESH)

    for c in loads[:4]:
        c.wait()

    gain_row = gain[pl.ds(ts[0], 1), :]
    rows = []
    for a in range(2):
        t = cot[pl.ds(64 * a, 16), :].astype(F32)
        for i in range(1, 4):
            t = t + cot[pl.ds(64 * a + 16 * i, 16), :].astype(F32)
        rows.append([jnp.sum(t[4 * m : 4 * m + 4], axis=0, keepdims=True) * gain_row for m in range(4)])
    pooled = jnp.concatenate(
        [
            jnp.concatenate([rows[0][2 * c], rows[0][2 * c + 1], rows[1][2 * c], rows[1][2 * c + 1]], axis=1)
            for c in range(2)
        ],
        axis=0,
    )
    half = lax.broadcasted_iota(jnp.int32, (2, 1024), 1) % 128 < 64
    kv_all = ckv[...].astype(F32)
    for part, (one, two) in enumerate(((cq[...].astype(F32), kv_all[:, :1024]), (kv_all[:, 1024:], pooled))):
        even = jnp.where(half, one, pltpu.roll(two, 64, 1)).astype(BF)
        odd = jnp.where(half, pltpu.roll(one, 1024 - 64, 1), two).astype(BF)
        for j in range(8):
            stage[2 * j, part] = even[:, 128 * j : 128 * j + 128]
            stage[2 * j + 1, part] = odd[:, 128 * j : 128 * j + 128]

    pl.semaphore_wait(barrier, len(peers))

    def a2a(k):
        there = lax.rem(f + k, F)
        return pltpu.make_async_remote_copy(
            src_ref=stage.at[there], dst_ref=land.at[:, f],
            send_sem=a2a_s.at[k - 1], recv_sem=a2a_r.at[k - 1],
            device_id=(there, r), device_id_type=MESH,
        )

    def a2a_in(k):
        here = lax.rem(f + F - k, F)
        return pltpu.make_async_remote_copy(
            src_ref=stage.at[here], dst_ref=land.at[:, here],
            send_sem=a2a_s.at[k - 1], recv_sem=a2a_r.at[k - 1],
            device_id=(here, r), device_id_type=MESH,
        )

    for k in range(1, F):
        a2a(k).start()
    own = pltpu.make_async_copy(stage.at[f], land.at[:, f], self_sem)
    own.start()

    halos = [
        pltpu.make_async_remote_copy(
            src_ref=fkv_h.at[pl.ds(PIX - HALO, HALO)], dst_ref=kv.at[pl.ds(0, HALO)],
            send_sem=halo_s.at[0], recv_sem=halo_r.at[0], device_id=below, device_id_type=MESH,
        ),
        pltpu.make_async_remote_copy(
            src_ref=fkv_h.at[pl.ds(0, HALO)], dst_ref=kv.at[pl.ds(HALO + PIX, HALO)],
            send_sem=halo_s.at[1], recv_sem=halo_r.at[1], device_id=above, device_id_type=MESH,
        ),
    ]
    for c in halos:
        c.start()

    own.wait()
    for k in range(1, F):
        a2a_in(k).wait_recv()
    for part in range(2):
        for i in range(F):
            buf[part, 0, 2 * i : 2 * i + 2, :] = land[part, i]

    children, order = tree()

    def pass_z(d, c):
        return pltpu.make_async_remote_copy(
            src_ref=buf.at[:, d % NZ], dst_ref=buf.at[:, c % NZ],
            send_sem=z_s.at[c % NZ], recv_sem=z_r.at[c % NZ],
            device_id=zdev(c - d), device_id_type=MESH,
        )

    def pass_x(d):
        return pltpu.make_async_remote_copy(
            src_ref=buf.at[:, d % NZ], dst_ref=buf.at[:, NZ + d % NZ],
            send_sem=x_s.at[d % NZ], recv_sem=x_r.at[d % NZ],
            device_id=xdev, device_id_type=MESH,
        )

    parent = {c: d for d, cs in children.items() for c in cs}

    def hand_on(d):
        for c in children.get(d, []):
            pass_z(d, c).start()
        pass_x(d).start()

    def arrive(d):
        pass_z(parent[d], d).wait_recv()
        hand_on(d)

    lane = lax.broadcasted_iota(jnp.int32, (PIX, 128), 1)

    def fine_prepare():
        for c in loads[4:]:
            c.wait()
        for c in halos:
            c.wait_recv()
        for p in range(2):
            cols = slice(128 * p, 128 * p + 128)
            q = fq[:, cols].astype(F32) * 0.125
            g = cot[:, cols].astype(F32) * gain_row[:, cols]
            for e in range(2):
                mine = lane < 64 if e == 0 else lane >= 64
                gs[0, p, pl.ds(PIX * e, PIX), :] = jnp.where(mine, q, 0.0).astype(BF)
                gs[1, p, pl.ds(PIX * e, PIX), :] = jnp.where(mine, g, 0.0).astype(BF)

    def fine_pair(p):
        qs = gs[0, p]
        g = gs[1, p]
        keys = kv[:, 128 * p : 128 * p + 128]
        values = kv[:, 256 + 128 * p : 256 + 128 * p + 128]
        qi = lax.broadcasted_iota(jnp.int32, (2 * PIX, KEYS), 0) % PIX
        ki = lax.broadcasted_iota(jnp.int32, (2 * PIX, KEYS), 1)
        dr = ki // 16 - 3 - qi // 16
        kc = ki % 16
        dc = kc - qi % 16
        row = r * 8 + ki // 16 - 3
        near = (jnp.abs(dr) <= 3) & (jnp.abs(dc) <= 3) & (row >= 0) & (row < ROWS * 8) & (kc < vc[f])
        near = near | ((dr == 0) & (dc == 0))
        s = jnp.where(near, dot(qs, keys, 1, 1), NEG)
        top = jnp.max(s, axis=1, keepdims=True)
        e = jnp.exp(s - top)
        w = e / jnp.sum(e, axis=1, keepdims=True)
        low = w.astype(BF)
        out = dot(low, values, 1, 0)
        row_dot = jnp.sum(g.astype(F32) * out, axis=1, keepdims=True)
        wg = dot(g, values, 1, 1)
        sg = (w * (wg - row_dot)).astype(BF)
        dq = dot(sg, keys, 1, 0) * 0.125
        o_fq[:, 128 * p : 128 * p + 128] = jnp.where(lane < 64, dq[:PIX], dq[PIX:]).astype(BF)
        dkv[:, 128 * p : 128 * p + 128] = dot(sg, qs, 0, 0)
        dkv[:, 256 + 128 * p : 256 + 128 * p + 128] = dot(low, g, 0, 0)

    rims = [
        pltpu.make_async_remote_copy(
            src_ref=rim_out.at[0], dst_ref=rim_in.at[0],
            send_sem=rim_s.at[0], recv_sem=rim_r.at[0], device_id=above, device_id_type=MESH,
        ),
        pltpu.make_async_remote_copy(
            src_ref=rim_out.at[1], dst_ref=rim_in.at[1],
            send_sem=rim_s.at[1], recv_sem=rim_r.at[1], device_id=below, device_id_type=MESH,
        ),
    ]
    fine_out = [
        pltpu.make_async_copy(o_fq, dfq_h, out_sem.at[0]),
        pltpu.make_async_copy(o_fkv, dfkv_h, out_sem.at[1]),
    ]

    def fine_send():
        rim_out[0] = dkv[pl.ds(0, HALO), :].astype(BF)
        rim_out[1] = dkv[pl.ds(HALO + PIX, HALO), :].astype(BF)
        for c in rims:
            c.start()
        fine_out[0].start()

    def fine_finish():
        for c in rims:
            c.wait_recv()
        mid = PIX - 2 * HALO
        o_fkv[pl.ds(0, HALO), :] = (dkv[pl.ds(HALO, HALO), :] + rim_in[1].astype(F32)).astype(BF)
        o_fkv[pl.ds(HALO, mid), :] = dkv[pl.ds(2 * HALO, mid), :].astype(BF)
        o_fkv[pl.ds(HALO + mid, HALO), :] = (
            dkv[pl.ds(2 * HALO + mid, HALO), :] + rim_in[0].astype(F32)
        ).astype(BF)
        fine_out[1].start()

    work = {1: [fine_prepare], 3: [functools.partial(fine_pair, 0)], -3: [],
            -4: [functools.partial(fine_pair, 1), fine_send], -10: [fine_finish]}

    hand_on(0)
    for d in order:
        arrive(d)
        for piece in work.get(d, []):
            piece()
    for d in [0] + order:
        pass_x(d).wait_recv()

    tl = lax.broadcasted_iota(jnp.int32, (32, 128), 1)
    ti = lax.broadcasted_iota(jnp.int32, (32, 128), 0)
    limit = jnp.zeros((32, 128), jnp.int32)
    for i in range(F):
        limit = jnp.where(ti // 2 == i, vc[i], limit)
    bias = jnp.where((tl == 0) & ((ti % 2) * 8 >= limit), NEG, 0.0).astype(F32)
    unit = jnp.where(tl == 0, 1.0, 0.0).astype(F32)
    bias3 = jnp.broadcast_to(bias[None], (8, 32, 128)).reshape(256, 128)
    unit3 = jnp.broadcast_to(unit[None], (8, 32, 128)).reshape(256, 128)
    upper = lax.broadcasted_iota(jnp.int32, (256, 128), 1) >= 64
    for i in range(8):
        at = pl.ds(256 * i, 256)
        qk = buf[0, 8 * i : 8 * i + 8].reshape(256, 128).astype(F32)
        a_ref[at, :] = jnp.where(upper, qk * 0.125, bias3).astype(BF)
        b_ref[at, :] = jnp.where(upper, pltpu.roll(qk, 64, 1), unit3).astype(BF)
        vg = buf[1, 8 * i : 8 * i + 8].reshape(256, 128).astype(F32)
        t_ref[:, 256 * i : 256 * i + 256] = jnp.transpose(vg, (1, 0)).astype(BF)

    def tile(i, carry):
        at = pl.multiple_of(i * QT, QT)
        s = dot(a_ref[...], b_ref[pl.ds(at, QT), :], 1, 1)
        top = jnp.max(s, axis=0, keepdims=True)
        e = jnp.exp(s - top)
        total = jnp.sum(e, axis=0, keepdims=True)
        out = dot(t_ref[pl.ds(0, 64), :], e.astype(BF), 1, 0)
        g = t_ref[pl.ds(64, 64), pl.ds(at, QT)].astype(F32)
        ld[0:1, pl.ds(at, QT)] = top + jnp.log(total)
        ld[1:2, pl.ds(at, QT)] = jnp.sum(g * out, axis=0, keepdims=True) / total
        return carry

    lax.fori_loop(0, TOK // QT, tile, 0)

    qk = buf[0].reshape(TOK, 128)
    vg = buf[1].reshape(TOK, 128)
    vt = t_ref[pl.ds(0, 64), :]
    gt = t_ref[pl.ds(64, 64), :]
    mine = buf[1, 0].astype(F32)
    v_own = mine[:, :64].astype(BF)
    g_wide = pltpu.roll(mine, 64, 1)[:, :64]
    g_own = g_wide.astype(BF)

    s = dot(a_ref[0:32, :], b_ref[...], 1, 1)
    w = jnp.exp(s - ld[0:1, :])
    dw = dot(v_own, gt, 1, 0)
    sg = (w * (dw - ld[1:2, :])).astype(BF)
    o_v[...] = dot(w.astype(BF), vg, 1, 0)[:, 64:].astype(BF)
    o_k[...] = (dot(sg, qk, 1, 0)[:, :64] * 0.125).astype(BF)

    s = dot(b_ref[0:32, :], a_ref[...], 1, 1)
    top = jnp.max(s, axis=1, keepdims=True)
    e = jnp.exp(s - top)
    w = e / jnp.sum(e, axis=1, keepdims=True)
    out = dot(w.astype(BF), vg, 1, 0)[:, :64]
    row_dot = jnp.sum(g_wide * out, axis=1, keepdims=True)
    dw = dot(g_own, vt, 1, 0)
    sg = (w * (dw - row_dot)).astype(BF)
    o_q[...] = (dot(sg, qk, 1, 0)[:, 64:] * 0.125).astype(BF)

    outs = [
        pltpu.make_async_copy(o_q, dq_h, out_sem.at[2]),
        pltpu.make_async_copy(o_k, dk_h, out_sem.at[3]),
        pltpu.make_async_copy(o_v, dv_h, out_sem.at[4]),
    ]
    for c in outs:
        c.start()
    for k in range(1, F):
        a2a(k).wait_send()
    for c in halos + rims:
        c.wait_send()
    for d in order:
        pass_z(parent[d], d).wait_send()
    for d in [0] + order:
        pass_x(d).wait_send()
    for c in fine_out + outs:
        c.wait()


def local(fine_q, fine_kv, coarse_q, coarse_kv, cotangent, gain_table, timesteps, valid_cols):
    smem = pl.BlockSpec(memory_space=pltpu.SMEM)
    hbm = pl.BlockSpec(memory_space=pl.ANY)
    vmem = pltpu.VMEM
    dma = pltpu.SemaphoreType.DMA
    dfq, dfkv, dq, dk, dv = pl.pallas_call(
        kernel,
        out_shape=(
            jax.ShapeDtypeStruct((PIX, 256), BF),
            jax.ShapeDtypeStruct((PIX, 512), BF),
            jax.ShapeDtypeStruct((32, 64), BF),
            jax.ShapeDtypeStruct((32, 64), BF),
            jax.ShapeDtypeStruct((32, 64), BF),
        ),
        in_specs=[smem, smem] + [hbm] * 6,
        out_specs=(hbm,) * 5,
        scratch_shapes=[
            vmem((PIX, 256), BF), vmem((KEYS, 512), BF), vmem((PIX, 256), BF),
            vmem((2, 1024), BF), vmem((2, 2048), BF), vmem((1000, 256), F32),
            vmem((F, 2, 2, 128), BF), vmem((2, F, 2, 128), BF), vmem((2, 2 * NZ, 32, 128), BF),
            vmem((2, 2, 2 * PIX, 128), BF), vmem((KEYS, 512), F32),
            vmem((2, HALO, 512), BF), vmem((2, HALO, 512), BF),
            vmem((TOK, 128), BF), vmem((TOK, 128), BF), vmem((128, TOK), BF), vmem((8, TOK), F32),
            vmem((PIX, 256), BF), vmem((PIX, 512), BF),
            vmem((32, 64), BF), vmem((32, 64), BF), vmem((32, 64), BF),
            dma((6,)), dma((5,)), dma((2,)), dma((2,)), dma((2,)), dma((2,)),
            dma((F - 1,)), dma((F - 1,)), dma,
            dma((NZ,)), dma((NZ,)), dma((NZ,)), dma((NZ,)),
        ],
        compiler_params=pltpu.CompilerParams(
            collective_id=0, has_side_effects=True, vmem_limit_bytes=48 * 1024 * 1024
        ),
    )(
        timesteps, valid_cols,
        fine_q.reshape(PIX, 256), fine_kv.reshape(PIX, 512), cotangent.reshape(PIX, 256),
        coarse_q.reshape(2, 1024), coarse_kv.reshape(2, 2048), gain_table,
    )
    return (
        dfq.reshape(1, 8, 16, 256), dfkv.reshape(1, 8, 16, 512),
        dq.reshape(F, 1, 2, 64), dk.reshape(F, 1, 2, 64), dv.reshape(F, 1, 2, 64),
    )


def solution(mesh):
    placed = P("frames", "rows", None, None)
    heads = P(None, "rows", None, "frames")
    return jax.shard_map(
        local,
        mesh=mesh,
        in_specs=(placed, placed, placed, placed, placed, P(), P("frames"), P()),
        out_specs=(placed, placed, heads, heads, heads),
        check_vma=False,
    )
```

time: 572 us -> 80.8 us (0.14)
  the two profiles are of different devices: /device:TPU:8 before, /device:TPU:2 now
where the time goes in v1:
time: 80.8 us; the launch traced here: 80.4 us
  Pallas kernels  70.9 us (88%)
  local copies, waits for them, and re-layouts  8.21 us (10%)
  between operations  1.32 us (2%)
    pallas_call x1, Pallas kernels, local(): pl.pallas_call(kernel, out_shape=(jax.ShapeDtypeStruct((PIX, 256), BF), j...  70.9 us
    unnamed x19, local copies, waits for them, and re-layouts  8.21 us

profile of v1, /device:TPU:2, one launch (start us, length us, event | category | flops | bytes accessed | tf_op | source)
XLA Modules:
  0.0 80.4 jit_solution(13882772363610490666)
XLA Ops:
  0.6 0.0 copy-start.4
  1.3 0.0 copy-start.6
  1.3 0.0 copy-done.4
  1.3 0.6 copy-done.6
  2.0 0.0 copy-start
  2.0 1.2 %copy-done = f32[1000,256]{1,0:T(8,128)S(1)} copy-done((f32[1000,256]{1,0:T(8,128)S(1)}, f32[1000,256]{1,0:T(8,128)}, u32[]{:S(2)}) %copy-start) | copy-done | bytes 1024024
  3.2 0.0 copy-start.1
  3.2 0.9 %copy-done.1 = bf16[1,8,16,512]{3,2,1,0:T(8,128)(2,1)S(1)} copy-done((bf16[1,8,16,512]{3,2,1,0:T(8,128)(2,1)S(1)}, bf16[1,8,16,512]{3,2,1,0:T(8,128)(2,1)}, u32[]{:S(2)}) %copy-start.1) | copy-done | bytes 131096
  4.1 0.0 copy-start.2
  4.1 0.8 %copy-done.2 = bf16[1,8,16,256]{3,2,1,0:T(8,128)(2,1)S(1)} copy-done((bf16[1,8,16,256]{3,2,1,0:T(8,128)(2,1)S(1)}, bf16[1,8,16,256]{3,2,1,0:T(8,128)(2,1)}, u32[]{:S(2)}) %copy-start.2) | copy-done | bytes 65560
  4.9 0.0 copy-start.3
  4.9 0.8 %copy-done.3 = bf16[1,8,16,256]{3,2,1,0:T(8,128)(2,1)S(1)} copy-done((bf16[1,8,16,256]{3,2,1,0:T(8,128)(2,1)S(1)}, bf16[1,8,16,256]{3,2,1,0:T(8,128)(2,1)}, u32[]{:S(2)}) %copy-start.3) | copy-done | bytes 65560
  5.8 0.0 copy-start.5
  5.8 0.7 copy-done.5
  6.4 70.9 %shard_map.119 = (bf16[128,256]{1,0:T(8,128)(2,1)S(1)}, bf16[128,512]{1,0:T(8,128)(2,1)S(1)}, bf16[32,64]{1,0:T(8,128)(2,1)S(1)}, bf16[32,64]{1,0:T(8,128)(2,1)S(1)}, bf16[32,64]{1,0:T(8,128)(2,1)S(1)}) custom-call(s32[1]{0:T(128)S(6)} %copy.21.ts, s32[16]{0:T(128)S(1)} %copy-done.6, bf16[128,256]{1,0:T(8,128)(2,1)S(1)} %bitcast.18, ...), custom_call_target="tpu_custom_call" | custom-call | tf_op jit(solution)/shard_map/pallas_call | solution.py:354
  77.3 0.6 copy.22
  78.0 0.7 copy.23
  78.6 0.6 copy.24
  79.2 0.6 copy.25
  79.8 0.6 copy.26
Async XLA Ops:
  0.6 0.7 copy-start.4
  1.3 0.7 copy-start.6
  2.0 1.2 %copy-start = (f32[1000,256]{1,0:T(8,128)S(1)}, f32[1000,256]{1,0:T(8,128)}, u32[]{:S(2)}) copy-start(f32[1000,256]{1,0:T(8,128)} %gain_h.1) | copy-start | bytes 3072004
  3.2 0.9 %copy-start.1 = (bf16[1,8,16,512]{3,2,1,0:T(8,128)(2,1)S(1)}, bf16[1,8,16,512]{3,2,1,0:T(8,128)(2,1)}, u32[]{:S(2)}) copy-start(bf16[1,8,16,512]{3,2,1,0:T(8,128)(2,1)} %param.9) | copy-start | bytes 393220
  4.1 0.8 %copy-start.2 = (bf16[1,8,16,256]{3,2,1,0:T(8,128)(2,1)S(1)}, bf16[1,8,16,256]{3,2,1,0:T(8,128)(2,1)}, u32[]{:S(2)}) copy-start(bf16[1,8,16,256]{3,2,1,0:T(8,128)(2,1)} %param.8) | copy-start | bytes 196612
  4.9 0.8 %copy-start.3 = (bf16[1,8,16,256]{3,2,1,0:T(8,128)(2,1)S(1)}, bf16[1,8,16,256]{3,2,1,0:T(8,128)(2,1)}, u32[]{:S(2)}) copy-start(bf16[1,8,16,256]{3,2,1,0:T(8,128)(2,1)} %param.12) | copy-start | bytes 196612
  5.8 0.7 copy-start.5

commit v2 on v1

--- a/solution.py
+++ b/solution.py
@@ -15,6 +15,7 @@
 KEYS = PIX + 2 * HALO
 TOK = 2048
 QT = 256
+KT = 128
 NEG = -1e30
 BF = jnp.bfloat16
 F32 = jnp.float32
@@ -22,18 +23,18 @@
 
 
 def tree():
-    children = {0: [3, -3, 1, -1]}
-    for k in (3, 6, 9, 12):
-        children[k] = [k + 3, k - 1, k + 1]
-        children[-k] = [-k - 3, -k + 1, -k - 1]
-    children[15] = [16, 14]
-    children[-15] = [-14]
+    children = {0: [5, -5, 1, -1, 2, -2]}
+    for k in (5, 10):
+        children[k] = [k + 5, k - 1, k + 1, k - 2, k + 2]
+        children[-k] = [-k - 5, -k + 1, -k - 1, -k + 2, -k - 2]
+    children[15] = [16, 14, 13]
+    children[-15] = [-14, -13]
     cost = {0: 0.0}
     todo = [0]
     while todo:
         d = todo.pop(0)
         for c in children.get(d, []):
-            cost[c] = cost[d] + 0.88 + 0.75 * abs(c - d)
+            cost[c] = cost[d] + 2.0 + 0.6 * abs(c - d)
             todo.append(c)
     order = sorted((d for d in cost if d), key=lambda d: (cost[d], -d))
     return children, order
@@ -47,7 +48,7 @@
     ts, vc, fq_h, fkv_h, cot_h, cq_h, ckv_h, gain_h,
     dfq_h, dfkv_h, dq_h, dk_h, dv_h,
     fq, kv, cot, cq, ckv, gain, stage, land, buf,
-    gs, dkv, rim_out, rim_in, a_ref, b_ref, t_ref, ld,
+    gs, dkv, rim_out, rim_in, a_ref, b_ref, t_ref, g_ref, top_ref, sum_ref, dot_ref, bias_ref,
     o_fq, o_fkv, o_q, o_k, o_v,
     in_sem, out_sem, halo_s, halo_r, rim_s, rim_r, a2a_s, a2a_r, self_sem,
     z_s, z_r, x_s, x_r,
@@ -63,6 +64,9 @@
     xdev = (f, (1 - xl) * NZ + z)
     above = (f, lax.rem(r + ROWS - 1, ROWS))
     below = (f, lax.rem(r + 1, ROWS))
+
+    children, order = tree()
+    slots = {d: 2 * i for i, d in enumerate([0] + order)}
 
     loads = [
         pltpu.make_async_copy(src, dst, in_sem.at[i])
@@ -82,7 +86,7 @@
 
     barrier = pltpu.get_barrier_semaphore()
     peers = [(lax.rem(f + k, F), r) for k in range(1, F)]
-    peers += [zdev(1), zdev(-1), zdev(3), zdev(-3), xdev, above, below]
+    peers += [zdev(1), zdev(-1), zdev(2), zdev(-2), zdev(5), zdev(-5), xdev, above, below]
     for peer in peers:
         pl.semaphore_signal(barrier, inc=1, device_id=peer, device_id_type=MESH)
 
@@ -155,18 +159,17 @@
         for i in range(F):
             buf[part, 0, 2 * i : 2 * i + 2, :] = land[part, i]
 
-    children, order = tree()
 
     def pass_z(d, c):
         return pltpu.make_async_remote_copy(
-            src_ref=buf.at[:, d % NZ], dst_ref=buf.at[:, c % NZ],
+            src_ref=buf.at[:, slots[d]], dst_ref=buf.at[:, slots[c]],
             send_sem=z_s.at[c % NZ], recv_sem=z_r.at[c % NZ],
             device_id=zdev(c - d), device_id_type=MESH,
         )
 
     def pass_x(d):
         return pltpu.make_async_remote_copy(
-            src_ref=buf.at[:, d % NZ], dst_ref=buf.at[:, NZ + d % NZ],
+            src_ref=buf.at[:, slots[d]], dst_ref=buf.at[:, slots[d] + 1],
             send_sem=x_s.at[d % NZ], recv_sem=x_r.at[d % NZ],
             device_id=xdev, device_id_type=MESH,
         )
@@ -258,62 +261,79 @@
         ).astype(BF)
         fine_out[1].start()
 
-    work = {1: [fine_prepare], 3: [functools.partial(fine_pair, 0)], -3: [],
-            -4: [functools.partial(fine_pair, 1), fine_send], -10: [fine_finish]}
+    tl = lax.broadcasted_iota(jnp.int32, (32, 128), 1)
+    ti = lax.broadcasted_iota(jnp.int32, (32, 128), 0)
+
+    def coarse_prepare():
+        limit = jnp.zeros((32, 128), jnp.int32)
+        for i in range(F):
+            limit = jnp.where(ti // 2 == i, vc[i], limit)
+        bias = jnp.where((tl == 0) & ((ti % 2) * 8 >= limit), NEG, 0.0).astype(F32)
+        bias_ref[...] = jnp.broadcast_to(bias[None], (8, 32, 128)).reshape(QT, 128)
+        t_ref[pl.ds(64, 16), :] = jnp.ones((16, TOK), BF)
+
+    def pair(q, c):
+        qs, ks = pl.ds(QT * q, QT), pl.ds(KT * c, KT)
+        s = dot(a_ref[ks, :], b_ref[qs, :], 1, 1)
+        top = jnp.max(s, axis=0, keepdims=True)
+        e = jnp.exp(s - top).astype(BF)
+        out = dot(t_ref[:, ks], e, 1, 0)
+        top_ref[c : c + 1, qs] = top
+        sum_ref[c : c + 1, qs] = out[64:65]
+        dot_ref[c : c + 1, qs] = jnp.sum(out[:64] * g_ref[:, qs], axis=0, keepdims=True)
+
+    def coarse_tile(t):
+        for d in ([0] + order)[4 * t : 4 * t + 4]:
+            pass_x(d).wait_recv()
+        at = pl.ds(QT * t, QT)
+        upper = lax.broadcasted_iota(jnp.int32, (QT, 128), 1) >= 64
+        unit = (lax.broadcasted_iota(jnp.int32, (QT, 128), 1) == 0).astype(F32)
+        qk = buf[0, 8 * t : 8 * t + 8].reshape(QT, 128).astype(F32)
+        a_ref[at, :] = jnp.where(upper, qk * 0.125, bias_ref[...]).astype(BF)
+        b_ref[at, :] = jnp.where(upper, pltpu.roll(qk, 64, 1), unit).astype(BF)
+        vg = jnp.transpose(buf[1, 8 * t : 8 * t + 8].reshape(QT, 128).astype(F32), (1, 0))
+        t_ref[pl.ds(0, 64), at] = vg[:64].astype(BF)
+        g_ref[:, at] = vg[64:]
+        for i in range(t):
+            pair(i, 2 * t)
+            pair(i, 2 * t + 1)
+        for c in range(2 * t + 2):
+            pair(t, c)
+
+    def tiles(*ts_):
+        return [functools.partial(coarse_tile, t) for t in ts_]
+
+    work = {
+        2: [coarse_prepare],
+        -5: [fine_prepare, functools.partial(fine_pair, 0), functools.partial(fine_pair, 1), fine_send],
+        -10: tiles(0, 1, 2) + [fine_finish],
+        -15: tiles(3, 4, 5),
+    }
 
     hand_on(0)
     for d in order:
         arrive(d)
         for piece in work.get(d, []):
             piece()
-    for d in [0] + order:
-        pass_x(d).wait_recv()
-
-    tl = lax.broadcasted_iota(jnp.int32, (32, 128), 1)
-    ti = lax.broadcasted_iota(jnp.int32, (32, 128), 0)
-    limit = jnp.zeros((32, 128), jnp.int32)
-    for i in range(F):
-        limit = jnp.where(ti // 2 == i, vc[i], limit)
-    bias = jnp.where((tl == 0) & ((ti % 2) * 8 >= limit), NEG, 0.0).astype(F32)
-    unit = jnp.where(tl == 0, 1.0, 0.0).astype(F32)
-    bias3 = jnp.broadcast_to(bias[None], (8, 32, 128)).reshape(256, 128)
-    unit3 = jnp.broadcast_to(unit[None], (8, 32, 128)).reshape(256, 128)
-    upper = lax.broadcasted_iota(jnp.int32, (256, 128), 1) >= 64
-    for i in range(8):
-        at = pl.ds(256 * i, 256)
-        qk = buf[0, 8 * i : 8 * i + 8].reshape(256, 128).astype(F32)
-        a_ref[at, :] = jnp.where(upper, qk * 0.125, bias3).astype(BF)
-        b_ref[at, :] = jnp.where(upper, pltpu.roll(qk, 64, 1), unit3).astype(BF)
-        vg = buf[1, 8 * i : 8 * i + 8].reshape(256, 128).astype(F32)
-        t_ref[:, 256 * i : 256 * i + 256] = jnp.transpose(vg, (1, 0)).astype(BF)
-
-    def tile(i, carry):
-        at = pl.multiple_of(i * QT, QT)
-        s = dot(a_ref[...], b_ref[pl.ds(at, QT), :], 1, 1)
-        top = jnp.max(s, axis=0, keepdims=True)
-        e = jnp.exp(s - top)
-        total = jnp.sum(e, axis=0, keepdims=True)
-        out = dot(t_ref[pl.ds(0, 64), :], e.astype(BF), 1, 0)
-        g = t_ref[pl.ds(64, 64), pl.ds(at, QT)].astype(F32)
-        ld[0:1, pl.ds(at, QT)] = top + jnp.log(total)
-        ld[1:2, pl.ds(at, QT)] = jnp.sum(g * out, axis=0, keepdims=True) / total
-        return carry
-
-    lax.fori_loop(0, TOK // QT, tile, 0)
+    coarse_tile(6)
+    coarse_tile(7)
+
+    top = jnp.max(top_ref[...], axis=0, keepdims=True)
+    share = jnp.exp(top_ref[...] - top)
+    total = jnp.sum(share * sum_ref[...], axis=0, keepdims=True)
+    log_total = top + jnp.log(total)
+    dots = jnp.sum(share * dot_ref[...], axis=0, keepdims=True) / total
 
     qk = buf[0].reshape(TOK, 128)
     vg = buf[1].reshape(TOK, 128)
-    vt = t_ref[pl.ds(0, 64), :]
-    gt = t_ref[pl.ds(64, 64), :]
     mine = buf[1, 0].astype(F32)
     v_own = mine[:, :64].astype(BF)
     g_wide = pltpu.roll(mine, 64, 1)[:, :64]
-    g_own = g_wide.astype(BF)
 
     s = dot(a_ref[0:32, :], b_ref[...], 1, 1)
-    w = jnp.exp(s - ld[0:1, :])
-    dw = dot(v_own, gt, 1, 0)
-    sg = (w * (dw - ld[1:2, :])).astype(BF)
+    w = jnp.exp(s - log_total)
+    dw = dot(v_own, g_ref[...].astype(BF), 1, 0)
+    sg = (w * (dw - dots)).astype(BF)
     o_v[...] = dot(w.astype(BF), vg, 1, 0)[:, 64:].astype(BF)
     o_k[...] = (dot(sg, qk, 1, 0)[:, :64] * 0.125).astype(BF)
 
@@ -323,7 +343,7 @@
     w = e / jnp.sum(e, axis=1, keepdims=True)
     out = dot(w.astype(BF), vg, 1, 0)[:, :64]
     row_dot = jnp.sum(g_wide * out, axis=1, keepdims=True)
-    dw = dot(g_own, vt, 1, 0)
+    dw = dot(g_wide.astype(BF), t_ref[pl.ds(0, 64), :], 1, 0)
     sg = (w * (dw - row_dot)).astype(BF)
     o_q[...] = (dot(sg, qk, 1, 0)[:, 64:] * 0.125).astype(BF)
 
@@ -346,21 +366,31 @@
         c.wait()
 
 
+def placing(*refs):
+    sem = refs[-1]
+    copies = [pltpu.make_async_copy(refs[i], refs[5 + i], sem.at[i]) for i in range(5)]
+    for c in copies:
+        c.start()
+    for c in copies:
+        c.wait()
+
+
 def local(fine_q, fine_kv, coarse_q, coarse_kv, cotangent, gain_table, timesteps, valid_cols):
     smem = pl.BlockSpec(memory_space=pltpu.SMEM)
     hbm = pl.BlockSpec(memory_space=pl.ANY)
     vmem = pltpu.VMEM
     dma = pltpu.SemaphoreType.DMA
-    dfq, dfkv, dq, dk, dv = pl.pallas_call(
+    shapes = (
+        jax.ShapeDtypeStruct((PIX, 256), BF),
+        jax.ShapeDtypeStruct((PIX, 512), BF),
+        jax.ShapeDtypeStruct((32, 64), BF),
+        jax.ShapeDtypeStruct((32, 64), BF),
+        jax.ShapeDtypeStruct((32, 64), BF),
+    )
+    made = pl.pallas_call(
         kernel,
-        out_shape=(
-            jax.ShapeDtypeStruct((PIX, 256), BF),
-            jax.ShapeDtypeStruct((PIX, 512), BF),
-            jax.ShapeDtypeStruct((32, 64), BF),
-            jax.ShapeDtypeStruct((32, 64), BF),
-            jax.ShapeDtypeStruct((32, 64), BF),
-        ),
-        in_specs=[smem, smem] + [hbm] * 6,
+        out_shape=shapes,
+        in_specs=[smem, smem] + [pl.BlockSpec(memory_space=pltpu.HBM)] * 6,
         out_specs=(hbm,) * 5,
         scratch_shapes=[
             vmem((PIX, 256), BF), vmem((KEYS, 512), BF), vmem((PIX, 256), BF),
@@ -368,7 +398,8 @@
             vmem((F, 2, 2, 128), BF), vmem((2, F, 2, 128), BF), vmem((2, 2 * NZ, 32, 128), BF),
             vmem((2, 2, 2 * PIX, 128), BF), vmem((KEYS, 512), F32),
             vmem((2, HALO, 512), BF), vmem((2, HALO, 512), BF),
-            vmem((TOK, 128), BF), vmem((TOK, 128), BF), vmem((128, TOK), BF), vmem((8, TOK), F32),
+            vmem((TOK, 128), BF), vmem((TOK, 128), BF), vmem((80, TOK), BF), vmem((64, TOK), F32),
+            vmem((16, TOK), F32), vmem((16, TOK), F32), vmem((16, TOK), F32), vmem((QT, 128), F32),
             vmem((PIX, 256), BF), vmem((PIX, 512), BF),
             vmem((32, 64), BF), vmem((32, 64), BF), vmem((32, 64), BF),
             dma((6,)), dma((5,)), dma((2,)), dma((2,)), dma((2,)), dma((2,)),
@@ -376,13 +407,26 @@
             dma((NZ,)), dma((NZ,)), dma((NZ,)), dma((NZ,)),
         ],
         compiler_params=pltpu.CompilerParams(
-            collective_id=0, has_side_effects=True, vmem_limit_bytes=48 * 1024 * 1024
+            collective_id=0, has_side_effects=True, vmem_limit_bytes=24 * 1024 * 1024
         ),
     )(
         timesteps, valid_cols,
-        fine_q.reshape(PIX, 256), fine_kv.reshape(PIX, 512), cotangent.reshape(PIX, 256),
-        coarse_q.reshape(2, 1024), coarse_kv.reshape(2, 2048), gain_table,
+        *(
+            pltpu.with_memory_space_constraint(x, pltpu.HBM)
+            for x in (
+                fine_q.reshape(PIX, 256), fine_kv.reshape(PIX, 512), cotangent.reshape(PIX, 256),
+                coarse_q.reshape(2, 1024), coarse_kv.reshape(2, 2048), gain_table,
+            )
+        ),
     )
+    dfq, dfkv, dq, dk, dv = pl.pallas_call(
+        placing,
+        out_shape=shapes,
+        in_specs=[hbm] * 5,
+        out_specs=(pl.BlockSpec(memory_space=pltpu.HBM),) * 5,
+        scratch_shapes=[dma((5,))],
+        compiler_params=pltpu.CompilerParams(vmem_limit_bytes=1024 * 1024),
+    )(*made)
     return (
         dfq.reshape(1, 8, 16, 256), dfkv.reshape(1, 8, 16, 512),
         dq.reshape(F, 1, 2, 64), dk.reshape(F, 1, 2, 64), dv.reshape(F, 1, 2, 64),

time: 80.8 us -> 70 us (0.87)
  local copies, waits for them, and re-layouts: 8.21 us -> 0.65 us
  Pallas kernels: 70.9 us -> 67.7 us
    unnamed x19 -> x2, local copies, waits for them, and re-layouts: 8.21 us -> 0.65 us
    pallas_call x1 -> x2, Pallas kernels: 70.9 us -> 67.7 us  [the longest x1 67 us: local(): pl.pallas_call(kernel, out_shape=shapes, in_specs=[smem, smem] + [pl.Bloc...]
where the time goes in v2:
time: 70 us; the launch traced here: 69.8 us
  Pallas kernels  67.7 us (97%)
  between operations  1.46 us (2%)
    pallas_call x1, Pallas kernels, local(): pl.pallas_call(kernel, out_shape=shapes, in_specs=[smem, smem] + [pl.Bloc...  67 us

profile of v2, /device:TPU:2, one launch (start us, length us, event | category | flops | bytes accessed | tf_op | source)
XLA Modules:
  0.0 69.8 jit_solution(16403095727921886233)
XLA Ops:
  1.3 0.0 copy-start
  1.3 0.6 copy-done
  1.9 67.0 %shard_map.119 = (bf16[128,256]{1,0:T(8,128)(2,1)S(1)}, bf16[128,512]{1,0:T(8,128)(2,1)S(1)}, bf16[32,64]{1,0:T(8,128)(2,1)S(1)}, bf16[32,64]{1,0:T(8,128)(2,1)S(1)}, bf16[32,64]{1,0:T(8,128)(2,1)S(1)}) custom-call(s32[1]{0:T(128)S(6)} %copy.16.ts, s32[16]{0:T(128)S(1)} %copy-done, bf16[128,256]{1,0:T(8,128)(2,1)} %bitcast.17, bf16[128,512]{1,0:T(8,128)(2,1)} %bitcast.16, ...), custom_call_target="tpu_custom_call" | custom-call | tf_op jit(solution)/shard_map/pallas_call | solution.py:390
  68.9 0.7 %shard_map.120 = (bf16[128,256]{1,0:T(8,128)(2,1)}, bf16[128,512]{1,0:T(8,128)(2,1)}, bf16[32,64]{1,0:T(8,128)(2,1)}, bf16[32,64]{1,0:T(8,128)(2,1)}, bf16[32,64]{1,0:T(8,128)(2,1)}) custom-call(bf16[128,256]{1,0:T(8,128)(2,1)S(1)} %get-tuple-element.15.refs_0_, bf16[128,512]{1,0:T(8,128)(2,1)S(1)} %get-tuple-element.16.refs_1_, ...), custom_call_target="tpu_custom_call" | custom-call | tf_op jit(solution)/shard_map/pallas_call | solution.py:422
Async XLA Ops:
  1.3 0.7 copy-start

commit v3 on v2

--- a/solution.py
+++ b/solution.py
@@ -45,9 +45,9 @@
 
 
 def kernel(
-    ts, vc, fq_h, fkv_h, cot_h, cq_h, ckv_h, gain_h,
+    ts, vc_h, fq_h, fkv_h, cot_h, cq_h, ckv_h, gain_h,
     dfq_h, dfkv_h, dq_h, dk_h, dv_h,
-    fq, kv, cot, cq, ckv, gain, stage, land, buf,
+    vc, fq, kv, cot, cq, ckv, gain, stage, land, buf,
     gs, dkv, rim_out, rim_in, a_ref, b_ref, t_ref, g_ref, top_ref, sum_ref, dot_ref, bias_ref,
     o_fq, o_fkv, o_q, o_k, o_v,
     in_sem, out_sem, halo_s, halo_r, rim_s, rim_r, a2a_s, a2a_r, self_sem,
@@ -72,25 +72,26 @@
         pltpu.make_async_copy(src, dst, in_sem.at[i])
         for i, (src, dst) in enumerate(
             (
-                (cq_h, cq),
-                (ckv_h, ckv),
                 (gain_h, gain),
                 (cot_h, cot),
+                (ckv_h, ckv),
+                (cq_h, cq),
+                (vc_h, vc),
                 (fq_h, fq),
                 (fkv_h, kv.at[pl.ds(HALO, PIX)]),
             )
         )
     ]
-    for c in loads:
-        c.start()
-
     barrier = pltpu.get_barrier_semaphore()
     peers = [(lax.rem(f + k, F), r) for k in range(1, F)]
     peers += [zdev(1), zdev(-1), zdev(2), zdev(-2), zdev(5), zdev(-5), xdev, above, below]
     for peer in peers:
         pl.semaphore_signal(barrier, inc=1, device_id=peer, device_id_type=MESH)
 
-    for c in loads[:4]:
+    for c in loads:
+        c.start()
+
+    for c in loads[:5]:
         c.wait()
 
     gain_row = gain[pl.ds(ts[0], 1), :]
@@ -188,7 +189,7 @@
     lane = lax.broadcasted_iota(jnp.int32, (PIX, 128), 1)
 
     def fine_prepare():
-        for c in loads[4:]:
+        for c in loads[5:]:
             c.wait()
         for c in halos:
             c.wait_recv()
@@ -272,15 +273,31 @@
         bias_ref[...] = jnp.broadcast_to(bias[None], (8, 32, 128)).reshape(QT, 128)
         t_ref[pl.ds(64, 16), :] = jnp.ones((16, TOK), BF)
 
-    def pair(q, c):
-        qs, ks = pl.ds(QT * q, QT), pl.ds(KT * c, KT)
-        s = dot(a_ref[ks, :], b_ref[qs, :], 1, 1)
+    def score(q, c):
+        return dot(a_ref[pl.ds(KT * c, KT), :], b_ref[pl.ds(QT * q, QT), :], 1, 1)
+
+    def weigh(q, c, s):
         top = jnp.max(s, axis=0, keepdims=True)
-        e = jnp.exp(s - top).astype(BF)
-        out = dot(t_ref[:, ks], e, 1, 0)
-        top_ref[c : c + 1, qs] = top
+        top_ref[c : c + 1, pl.ds(QT * q, QT)] = top
+        return dot(t_ref[:, pl.ds(KT * c, KT)], jnp.exp(s - top).astype(BF), 1, 0)
+
+    def settle(q, c, out):
+        qs = pl.ds(QT * q, QT)
         sum_ref[c : c + 1, qs] = out[64:65]
         dot_ref[c : c + 1, qs] = jnp.sum(out[:64] * g_ref[:, qs], axis=0, keepdims=True)
+
+    def parts(todo):
+        depth = 8
+        scores = [score(*p) for p in todo[:depth]]
+        outs = []
+        for i, p in enumerate(todo):
+            if i + depth < len(todo):
+                scores.append(score(*todo[i + depth]))
+            outs.append(weigh(*p, scores[i]))
+            if i >= depth:
+                settle(*todo[i - depth], outs[i - depth])
+        for i in range(max(0, len(todo) - depth), len(todo)):
+            settle(*todo[i], outs[i])
 
     def coarse_tile(t):
         for d in ([0] + order)[4 * t : 4 * t + 4]:
@@ -294,11 +311,7 @@
         vg = jnp.transpose(buf[1, 8 * t : 8 * t + 8].reshape(QT, 128).astype(F32), (1, 0))
         t_ref[pl.ds(0, 64), at] = vg[:64].astype(BF)
         g_ref[:, at] = vg[64:]
-        for i in range(t):
-            pair(i, 2 * t)
-            pair(i, 2 * t + 1)
-        for c in range(2 * t + 2):
-            pair(t, c)
+        parts([(i, c) for i in range(t) for c in (2 * t, 2 * t + 1)] + [(t, c) for c in range(2 * t + 2)])
 
     def tiles(*ts_):
         return [functools.partial(coarse_tile, t) for t in ts_]
@@ -390,9 +403,10 @@
     made = pl.pallas_call(
         kernel,
         out_shape=shapes,
-        in_specs=[smem, smem] + [pl.BlockSpec(memory_space=pltpu.HBM)] * 6,
+        in_specs=[smem] + [pl.BlockSpec(memory_space=pltpu.HBM)] * 7,
         out_specs=(hbm,) * 5,
         scratch_shapes=[
+            pltpu.SMEM((F,), jnp.int32),
             vmem((PIX, 256), BF), vmem((KEYS, 512), BF), vmem((PIX, 256), BF),
             vmem((2, 1024), BF), vmem((2, 2048), BF), vmem((1000, 256), F32),
             vmem((F, 2, 2, 128), BF), vmem((2, F, 2, 128), BF), vmem((2, 2 * NZ, 32, 128), BF),
@@ -402,7 +416,7 @@
             vmem((16, TOK), F32), vmem((16, TOK), F32), vmem((16, TOK), F32), vmem((QT, 128), F32),
             vmem((PIX, 256), BF), vmem((PIX, 512), BF),
             vmem((32, 64), BF), vmem((32, 64), BF), vmem((32, 64), BF),
-            dma((6,)), dma((5,)), dma((2,)), dma((2,)), dma((2,)), dma((2,)),
+            dma((7,)), dma((5,)), dma((2,)), dma((2,)), dma((2,)), dma((2,)),
             dma((F - 1,)), dma((F - 1,)), dma,
             dma((NZ,)), dma((NZ,)), dma((NZ,)), dma((NZ,)),
         ],
@@ -410,10 +424,11 @@
             collective_id=0, has_side_effects=True, vmem_limit_bytes=24 * 1024 * 1024
         ),
     )(
-        timesteps, valid_cols,
+        timesteps,
         *(
             pltpu.with_memory_space_constraint(x, pltpu.HBM)
             for x in (
+                valid_cols,
                 fine_q.reshape(PIX, 256), fine_kv.reshape(PIX, 512), cotangent.reshape(PIX, 256),
                 coarse_q.reshape(2, 1024), coarse_kv.reshape(2, 2048), gain_table,
             )

time: 70 us -> 60.3 us (0.86)
  Pallas kernels: 67.7 us -> 58.8 us
    pallas_call x1, Pallas kernels: 67 us -> 58.1 us  [local(): pl.pallas_call(kernel, out_shape=shapes, in_specs=[smem] + [pl.BlockSpec(...]
where the time goes in v3:
time: 60.3 us; the launch traced here: 60.1 us
  Pallas kernels  58.8 us (98%)
  between operations  1.29 us (2%)
    pallas_call x1, Pallas kernels, local(): pl.pallas_call(kernel, out_shape=shapes, in_specs=[smem] + [pl.BlockSpec(...  58.1 us

profile of v3, /device:TPU:2, one launch (start us, length us, event | category | flops | bytes accessed | tf_op | source)
XLA Modules:
  0.0 60.1 jit_solution(11413222067886903704)
XLA Ops:
  1.3 58.1 %shard_map.119 = (bf16[128,256]{1,0:T(8,128)(2,1)S(1)}, bf16[128,512]{1,0:T(8,128)(2,1)S(1)}, bf16[32,64]{1,0:T(8,128)(2,1)S(1)}, bf16[32,64]{1,0:T(8,128)(2,1)S(1)}, bf16[32,64]{1,0:T(8,128)(2,1)S(1)}) custom-call(s32[1]{0:T(128)S(6)} %copy.16.ts, s32[16]{0:T(128)} %vc_h.1, bf16[128,256]{1,0:T(8,128)(2,1)} %bitcast.17, bf16[128,512]{1,0:T(8,128)(2,1)} %bitcast.16, ...), custom_call_target="tpu_custom_call" | custom-call | tf_op jit(solution)/shard_map/pallas_call | solution.py:403
  59.4 0.7 %shard_map.120 = (bf16[128,256]{1,0:T(8,128)(2,1)}, bf16[128,512]{1,0:T(8,128)(2,1)}, bf16[32,64]{1,0:T(8,128)(2,1)}, bf16[32,64]{1,0:T(8,128)(2,1)}, bf16[32,64]{1,0:T(8,128)(2,1)}) custom-call(bf16[128,256]{1,0:T(8,128)(2,1)S(1)} %get-tuple-element.15.refs_0_, bf16[128,512]{1,0:T(8,128)(2,1)S(1)} %get-tuple-element.16.refs_1_, ...), custom_call_target="tpu_custom_call" | custom-call | tf_op jit(solution)/shard_map/pallas_call | solution.py:437

commit v4 on v3

--- a/solution.py
+++ b/solution.py
@@ -22,15 +22,18 @@
 MESH = pl.DeviceIdType.MESH
 
 
+ROOTS = (0,)
+SHARED = (16, 14, -14)
+
+
 def tree():
-    children = {0: [5, -5, 1, -1, 2, -2]}
-    for k in (5, 10):
-        children[k] = [k + 5, k - 1, k + 1, k - 2, k + 2]
-        children[-k] = [-k - 5, -k + 1, -k - 1, -k + 2, -k - 2]
-    children[15] = [16, 14, 13]
-    children[-15] = [-14, -13]
-    cost = {0: 0.0}
-    todo = [0]
+    children = {0: [5, -5, 1, -1, 2, -2], 15: [16, 14], -15: [-14]}
+    for k in (5, -5, 10, -10):
+        sign = 1 if k > 0 else -1
+        hops = (5, -1, 1, -2, 2, 3) if abs(k) == 10 else (5, -1, 1, -2, 2)
+        children[k] = [k + sign * h for h in hops]
+    cost = {d: 4.4 + 0.6 * abs(d) for d in ROOTS}
+    todo = list(ROOTS)
     while todo:
         d = todo.pop(0)
         for c in children.get(d, []):
@@ -58,8 +61,8 @@
     xl = r // NZ
     z = lax.rem(r, NZ)
 
-    def zdev(d):
-        return (f, xl * NZ + lax.rem(z + d + NZ, NZ))
+    def zdev(d, head=f, column=xl):
+        return (head, column * NZ + lax.rem(z + d + NZ, NZ))
 
     xdev = (f, (1 - xl) * NZ + z)
     above = (f, lax.rem(r + ROWS - 1, ROWS))
@@ -67,6 +70,7 @@
 
     children, order = tree()
     slots = {d: 2 * i for i, d in enumerate([0] + order)}
+    parent = {c: d for d, cs in children.items() for c in cs}
 
     loads = [
         pltpu.make_async_copy(src, dst, in_sem.at[i])
@@ -83,8 +87,10 @@
         )
     ]
     barrier = pltpu.get_barrier_semaphore()
-    peers = [(lax.rem(f + k, F), r) for k in range(1, F)]
-    peers += [zdev(1), zdev(-1), zdev(2), zdev(-2), zdev(5), zdev(-5), xdev, above, below]
+    hops = sorted({c - d for d, cs in children.items() for c in cs} | {d - c for d, cs in children.items() for c in cs})
+    skew = sorted({s * (c - parent[c]) for c in SHARED for s in (1, -1)})
+    peers = [zdev(o, lax.rem(f + k, F)) for o in ROOTS for k in range(F) if o or k]
+    peers += [zdev(o) for o in hops] + [zdev(o, f, 1 - xl) for o in skew] + [xdev, above, below]
     for peer in peers:
         pl.semaphore_signal(barrier, inc=1, device_id=peer, device_id_type=MESH)
 
@@ -119,26 +125,29 @@
 
     pl.semaphore_wait(barrier, len(peers))
 
-    def a2a(k):
+    def a2a(o, k):
         there = lax.rem(f + k, F)
+        at = ROOTS.index(o)
         return pltpu.make_async_remote_copy(
-            src_ref=stage.at[there], dst_ref=land.at[:, f],
-            send_sem=a2a_s.at[k - 1], recv_sem=a2a_r.at[k - 1],
-            device_id=(there, r), device_id_type=MESH,
-        )
-
-    def a2a_in(k):
+            src_ref=stage.at[there], dst_ref=land.at[at, :, f],
+            send_sem=a2a_s.at[at, k], recv_sem=a2a_r.at[at, k],
+            device_id=zdev(o, there), device_id_type=MESH,
+        )
+
+    def a2a_in(o, k):
         here = lax.rem(f + F - k, F)
+        at = ROOTS.index(o)
         return pltpu.make_async_remote_copy(
-            src_ref=stage.at[here], dst_ref=land.at[:, here],
-            send_sem=a2a_s.at[k - 1], recv_sem=a2a_r.at[k - 1],
-            device_id=(here, r), device_id_type=MESH,
-        )
-
-    for k in range(1, F):
-        a2a(k).start()
-    own = pltpu.make_async_copy(stage.at[f], land.at[:, f], self_sem)
+            src_ref=stage.at[here], dst_ref=land.at[at, :, here],
+            send_sem=a2a_s.at[at, k], recv_sem=a2a_r.at[at, k],
+            device_id=zdev(-o, here), device_id_type=MESH,
+        )
+
+    sends = [(o, k) for o in ROOTS for k in range(F) if o or k]
+    own = pltpu.make_async_copy(stage.at[f], land.at[ROOTS.index(0), :, f], self_sem)
     own.start()
+    for o, k in sends:
+        a2a(o, k).start()
 
     halos = [
         pltpu.make_async_remote_copy(
@@ -153,13 +162,15 @@
     for c in halos:
         c.start()
 
-    own.wait()
-    for k in range(1, F):
-        a2a_in(k).wait_recv()
-    for part in range(2):
-        for i in range(F):
-            buf[part, 0, 2 * i : 2 * i + 2, :] = land[part, i]
-
+    def gather_heads(o):
+        if o == 0:
+            own.wait()
+        for k in range(F):
+            if o or k:
+                a2a_in(o, k).wait_recv()
+        for part in range(2):
+            for i in range(F):
+                buf[part, slots[o], 2 * i : 2 * i + 2, :] = land[ROOTS.index(o), part, i]
 
     def pass_z(d, c):
         return pltpu.make_async_remote_copy(
@@ -175,15 +186,30 @@
             device_id=xdev, device_id_type=MESH,
         )
 
-    parent = {c: d for d, cs in children.items() for c in cs}
+    def pass_both(c):
+        d = parent[c]
+        return pltpu.make_async_remote_copy(
+            src_ref=buf.at[:, slots[d]], dst_ref=buf.at[:, slots[c] + 1],
+            send_sem=x_s.at[c % NZ], recv_sem=x_r.at[c % NZ],
+            device_id=zdev(c - d, f, 1 - xl), device_id_type=MESH,
+        )
+
+    def other(d):
+        return pass_both(d) if d in SHARED else pass_x(d)
 
     def hand_on(d):
         for c in children.get(d, []):
             pass_z(d, c).start()
-        pass_x(d).start()
+            if c in SHARED:
+                pass_both(c).start()
+        if d not in SHARED:
+            pass_x(d).start()
 
     def arrive(d):
-        pass_z(parent[d], d).wait_recv()
+        if d in ROOTS:
+            gather_heads(d)
+        else:
+            pass_z(parent[d], d).wait_recv()
         hand_on(d)
 
     lane = lax.broadcasted_iota(jnp.int32, (PIX, 128), 1)
@@ -301,7 +327,7 @@
 
     def coarse_tile(t):
         for d in ([0] + order)[4 * t : 4 * t + 4]:
-            pass_x(d).wait_recv()
+            other(d).wait_recv()
         at = pl.ds(QT * t, QT)
         upper = lax.broadcasted_iota(jnp.int32, (QT, 128), 1) >= 64
         unit = (lax.broadcasted_iota(jnp.int32, (QT, 128), 1) == 0).astype(F32)
@@ -323,8 +349,7 @@
         -15: tiles(3, 4, 5),
     }
 
-    hand_on(0)
-    for d in order:
+    for d in [0] + order:
         arrive(d)
         for piece in work.get(d, []):
             piece()
@@ -367,14 +392,14 @@
     ]
     for c in outs:
         c.start()
-    for k in range(1, F):
-        a2a(k).wait_send()
+    for o, k in sends:
+        a2a(o, k).wait_send()
     for c in halos + rims:
         c.wait_send()
-    for d in order:
-        pass_z(parent[d], d).wait_send()
     for d in [0] + order:
-        pass_x(d).wait_send()
+        if d not in ROOTS:
+            pass_z(parent[d], d).wait_send()
+        other(d).wait_send()
     for c in fine_out + outs:
         c.wait()
 
@@ -409,7 +434,7 @@
             pltpu.SMEM((F,), jnp.int32),
             vmem((PIX, 256), BF), vmem((KEYS, 512), BF), vmem((PIX, 256), BF),
             vmem((2, 1024), BF), vmem((2, 2048), BF), vmem((1000, 256), F32),
-            vmem((F, 2, 2, 128), BF), vmem((2, F, 2, 128), BF), vmem((2, 2 * NZ, 32, 128), BF),
+            vmem((F, 2, 2, 128), BF), vmem((len(ROOTS), 2, F, 2, 128), BF), vmem((2, 2 * NZ, 32, 128), BF),
             vmem((2, 2, 2 * PIX, 128), BF), vmem((KEYS, 512), F32),
             vmem((2, HALO, 512), BF), vmem((2, HALO, 512), BF),
             vmem((TOK, 128), BF), vmem((TOK, 128), BF), vmem((80, TOK), BF), vmem((64, TOK), F32),
@@ -417,7 +442,7 @@
             vmem((PIX, 256), BF), vmem((PIX, 512), BF),
             vmem((32, 64), BF), vmem((32, 64), BF), vmem((32, 64), BF),
             dma((7,)), dma((5,)), dma((2,)), dma((2,)), dma((2,)), dma((2,)),
-            dma((F - 1,)), dma((F - 1,)), dma,
+            dma((len(ROOTS), F)), dma((len(ROOTS), F)), dma,
             dma((NZ,)), dma((NZ,)), dma((NZ,)), dma((NZ,)),
         ],
         compiler_params=pltpu.CompilerParams(

time: 60.3 us -> 57.6 us (0.955)
  the two profiles are of different devices: /device:TPU:2 before, /device:TPU:8 now
where the time goes in v4:
time: 57.6 us; the launch traced here: 57.4 us
  Pallas kernels  56.2 us (98%)
  between operations  1.29 us (2%)
    pallas_call x1, Pallas kernels, local(): pl.pallas_call(kernel, out_shape=shapes, in_specs=[smem] + [pl.BlockSpec(...  55.4 us

profile of v4, /device:TPU:8, one launch (start us, length us, event | category | flops | bytes accessed | tf_op | source)
XLA Modules:
  0.0 57.4 jit_solution(15401492151887275412)
XLA Ops:
  1.3 55.4 %shard_map.119 = (bf16[128,256]{1,0:T(8,128)(2,1)S(1)}, bf16[128,512]{1,0:T(8,128)(2,1)S(1)}, bf16[32,64]{1,0:T(8,128)(2,1)S(1)}, bf16[32,64]{1,0:T(8,128)(2,1)S(1)}, bf16[32,64]{1,0:T(8,128)(2,1)S(1)}) custom-call(s32[1]{0:T(128)S(6)} %copy.16.ts, s32[16]{0:T(128)} %vc_h.1, bf16[128,256]{1,0:T(8,128)(2,1)} %bitcast.17, bf16[128,512]{1,0:T(8,128)(2,1)} %bitcast.16, ...), custom_call_target="tpu_custom_call" | custom-call | tf_op jit(solution)/shard_map/pallas_call | solution.py:428
  56.7 0.7 %shard_map.120 = (bf16[128,256]{1,0:T(8,128)(2,1)}, bf16[128,512]{1,0:T(8,128)(2,1)}, bf16[32,64]{1,0:T(8,128)(2,1)}, bf16[32,64]{1,0:T(8,128)(2,1)}, bf16[32,64]{1,0:T(8,128)(2,1)}) custom-call(bf16[128,256]{1,0:T(8,128)(2,1)S(1)} %get-tuple-element.15.refs_0_, bf16[128,512]{1,0:T(8,128)(2,1)S(1)} %get-tuple-element.16.refs_1_, ...), custom_call_target="tpu_custom_call" | custom-call | tf_op jit(solution)/shard_map/pallas_call | solution.py:462

commit v5 on v4

--- a/solution.py
+++ b/solution.py
@@ -27,10 +27,13 @@
 
 
 def tree():
-    children = {0: [5, -5, 1, -1, 2, -2], 15: [16, 14], -15: [-14]}
+    children = {0: [5, -5, 1, -1], 15: [16, 14], -15: [-14], 1: [2], -1: [-2]}
     for k in (5, -5, 10, -10):
         sign = 1 if k > 0 else -1
-        hops = (5, -1, 1, -2, 2, 3) if abs(k) == 10 else (5, -1, 1, -2, 2)
+        hops = (5, -1, 1, -2, 2, 3) if abs(k) == 10 else (5, -1, 1)
+        if abs(k) == 5:
+            children[k + 1] = [k + 2]
+            children[k - 1] = [k - 2]
         children[k] = [k + sign * h for h in hops]
     cost = {d: 4.4 + 0.6 * abs(d) for d in ROOTS}
     todo = list(ROOTS)

time: 57.6 us -> 57 us (0.990)
  Pallas kernels: 56.2 us -> 55.6 us
    pallas_call x1, Pallas kernels: 55.4 us -> 54.8 us  [local(): pl.pallas_call(kernel, out_shape=shapes, in_specs=[smem] + [pl.BlockSpec(...]
where the time goes in v5:
time: 57 us; the launch traced here: 56.9 us
  Pallas kernels  55.6 us (98%)
  between operations  1.29 us (2%)
    pallas_call x1, Pallas kernels, local(): pl.pallas_call(kernel, out_shape=shapes, in_specs=[smem] + [pl.BlockSpec(...  54.8 us

profile of v5, /device:TPU:8, one launch (start us, length us, event | category | flops | bytes accessed | tf_op | source)
XLA Modules:
  0.0 56.9 jit_solution(3180789810063365706)
XLA Ops:
  1.3 54.8 %shard_map.119 = (bf16[128,256]{1,0:T(8,128)(2,1)S(1)}, bf16[128,512]{1,0:T(8,128)(2,1)S(1)}, bf16[32,64]{1,0:T(8,128)(2,1)S(1)}, bf16[32,64]{1,0:T(8,128)(2,1)S(1)}, bf16[32,64]{1,0:T(8,128)(2,1)S(1)}) custom-call(s32[1]{0:T(128)S(6)} %copy.16.ts, s32[16]{0:T(128)} %vc_h.1, bf16[128,256]{1,0:T(8,128)(2,1)} %bitcast.17, bf16[128,512]{1,0:T(8,128)(2,1)} %bitcast.16, ...), custom_call_target="tpu_custom_call" | custom-call | tf_op jit(solution)/shard_map/pallas_call | solution.py:431
  56.1 0.7 %shard_map.120 = (bf16[128,256]{1,0:T(8,128)(2,1)}, bf16[128,512]{1,0:T(8,128)(2,1)}, bf16[32,64]{1,0:T(8,128)(2,1)}, bf16[32,64]{1,0:T(8,128)(2,1)}, bf16[32,64]{1,0:T(8,128)(2,1)}) custom-call(bf16[128,256]{1,0:T(8,128)(2,1)S(1)} %get-tuple-element.15.refs_0_, bf16[128,512]{1,0:T(8,128)(2,1)S(1)} %get-tuple-element.16.refs_1_, ...), custom_call_target="tpu_custom_call" | custom-call | tf_op jit(solution)/shard_map/pallas_call | solution.py:465

commit v6 on v5

--- a/solution.py
+++ b/solution.py
@@ -202,9 +202,9 @@
 
     def hand_on(d):
         for c in children.get(d, []):
-            pass_z(d, c).start()
             if c in SHARED:
                 pass_both(c).start()
+            pass_z(d, c).start()
         if d not in SHARED:
             pass_x(d).start()
 

time: 57 us -> 57.2 us (level)
  no operation moved by 1% of the time
where the time goes in v6:
time: 57.2 us; the launch traced here: 57 us
  Pallas kernels  55.7 us (97%)
  between operations  1.29 us (2%)
    pallas_call x1, Pallas kernels, local(): pl.pallas_call(kernel, out_shape=shapes, in_specs=[smem] + [pl.BlockSpec(...  55 us

profile of v6, /device:TPU:8, one launch (start us, length us, event | category | flops | bytes accessed | tf_op | source)
XLA Modules:
  0.0 57.0 jit_solution(721129329322630696)
XLA Ops:
  1.3 55.0 %shard_map.119 = (bf16[128,256]{1,0:T(8,128)(2,1)S(1)}, bf16[128,512]{1,0:T(8,128)(2,1)S(1)}, bf16[32,64]{1,0:T(8,128)(2,1)S(1)}, bf16[32,64]{1,0:T(8,128)(2,1)S(1)}, bf16[32,64]{1,0:T(8,128)(2,1)S(1)}) custom-call(s32[1]{0:T(128)S(6)} %copy.16.ts, s32[16]{0:T(128)} %vc_h.1, bf16[128,256]{1,0:T(8,128)(2,1)} %bitcast.17, bf16[128,512]{1,0:T(8,128)(2,1)} %bitcast.16, ...), custom_call_target="tpu_custom_call" | custom-call | tf_op jit(solution)/shard_map/pallas_call | solution.py:431
  56.3 0.7 %shard_map.120 = (bf16[128,256]{1,0:T(8,128)(2,1)}, bf16[128,512]{1,0:T(8,128)(2,1)}, bf16[32,64]{1,0:T(8,128)(2,1)}, bf16[32,64]{1,0:T(8,128)(2,1)}, bf16[32,64]{1,0:T(8,128)(2,1)}) custom-call(bf16[128,256]{1,0:T(8,128)(2,1)S(1)} %get-tuple-element.15.refs_0_, bf16[128,512]{1,0:T(8,128)(2,1)S(1)} %get-tuple-element.16.refs_1_, ...), custom_call_target="tpu_custom_call" | custom-call | tf_op jit(solution)/shard_map/pallas_call | solution.py:465
